TPU v7x, 32 devices: a whole 2x2x4 slice. The times are simulated.
32 devices in a mesh: lon: 4 (over x, core), frame: 8 (over z, y).
Axes of the slice: x: 2, y: 2, z: 4, core: 2. Of those that a mesh axis runs over, the one named last changes fastest.
Arguments:
- layer_input: bfloat16 [8, 16, 512, 128], P('frame', None, 'lon'), may hold values from -6 to 6
- hidden_saved: bfloat16 [8, 16, 512, 128], P('frame', None, 'lon'), as said below
- conv_weight: bfloat16 [3, 3, 128, 128], replicated, may hold values from -0.1875 to 0.1875
- queries: bfloat16 [2048, 128], P('lon'), may hold values from -6 to 6
- corr_cotangent: bfloat16 [8, 49, 2048], P('frame', None, 'lon'), may hold values from -0.59765625 to 0.59765625
- window_rows: int32 [8, 2048], P('frame', 'lon'), may hold values from 0 to 9
- window_cols: int32 [8, 2048], P('frame', 'lon'), may hold values from -3 to 124
- owner_strip: int32 [8, 2048, 1], P('frame', 'lon'), may hold values from 0 to 3; in each aligned block of 512 rows (0 to 511, 512 to 1023, ..., all dimensions but the last counted through in order) at most 128 rows name the same one
Outputs:
- query_grad: float32 [2048, 128], P(('lon', 'frame'))
- first_weight_grad: float32 [3, 3, 128, 128], replicated
- second_weight_grad: float32 [3, 3, 128, 128], replicated
Inputs may be any that keep to these rules, and one draw needn't show every extreme that they name: `hidden_saved`: rectifier outputs: zero or positive, a third or more of them exactly zero. `owner_strip`: in each frame, at most 128 of the 512 tracks homed on one strip name the same owning strip.
All inputs are finite; a program needn't handle non-finite values.
Results may differ from a plain program's by a relative error of at most 0.0045.
Values may be sent and summed in bfloat16 or wider, within the bound.
A program may use at most 64 MiB of HBM per device.

v0:
```python
import math
import jax
import jax.numpy as jnp
from jax import lax
from jax.sharding import PartitionSpec as P

WIN = 7


def padded_2(value, sides, width):
    for axis, dim in sides:
        peers, length = (lax.axis_size(axis), value.shape[dim])
        up = [(i, (i + 1) % peers) for i in range(peers)]
        down = [(j, i) for i, j in up]
        last = lax.slice_in_dim(value, length - width, length, axis=dim)
        first = lax.slice_in_dim(value, 0, width, axis=dim)
        before = lax.ppermute(last, axis, up)
        after = lax.ppermute(first, axis, down)
        value = jnp.concatenate([before, value, after], axis=dim)
    return value


def from_behind(value, axis, steps):
    count = lax.axis_size(axis)
    pairs = [(source, (source + steps) % count) for source in range(count)]
    return lax.ppermute(value, axis, pairs)


def pad_rows(field):
    return jnp.pad(field, ((1, 1), (0, 0), (0, 0)))


def conv_cells(padded, weight, out_cols):
    row_count = padded.shape[0] - 2
    result = jnp.zeros((row_count, out_cols, weight.shape[3]), jnp.float32)
    for row_tap in range(3):
        for col_tap in range(3):
            window = padded[row_tap : row_tap + row_count, col_tap : col_tap + out_cols]
            result = result + jnp.einsum(
                "rci,io->rco", window, weight[row_tap, col_tap], preferred_element_type=jnp.float32
            )
    return result


def conv_back(padded, weight, out_cols):
    row_count = padded.shape[0] - 2
    result = jnp.zeros((row_count, out_cols, weight.shape[2]), jnp.float32)
    for row_tap in range(3):
        for col_tap in range(3):
            window = padded[
                2 - row_tap : 2 - row_tap + row_count, 2 - col_tap : 2 - col_tap + out_cols
            ]
            result = result + jnp.einsum(
                "rco,io->rci", window, weight[row_tap, col_tap], preferred_element_type=jnp.float32
            )
    return result


def weight_terms(padded, grad):
    row_count, col_count, out_channels = grad.shape
    flat_grad = grad.reshape(row_count * col_count, out_channels)
    tap_terms = []
    for row_tap in range(3):
        for col_tap in range(3):
            window = padded[row_tap : row_tap + row_count, col_tap : col_tap + col_count].reshape(
                row_count * col_count, padded.shape[2]
            )
            tap_terms.append(
                lax.dot_general(
                    window, flat_grad, (((0,), (0,)), ((), ())), preferred_element_type=jnp.float32
                )
            )
    return jnp.stack(tap_terms).reshape(3, 3, padded.shape[2], out_channels)


def per_device(
    layer_input,
    hidden_saved,
    conv_weight,
    queries,
    corr_cotangent,
    window_rows,
    window_cols,
    owner_strip,
):
    strip_count = lax.axis_size("lon")
    input_local = layer_input[0]
    hidden_local = hidden_saved[0]
    row_count, col_count, channels = hidden_local.shape
    track_count = queries.shape[0]
    capacity = track_count // 4
    slot_count = strip_count * capacity
    wide_cols = col_count + 6
    taps_total = WIN * WIN
    reach = 4
    stacked = jnp.stack([input_local, hidden_local])
    edged = padded_2(stacked, (("lon", 2),), reach)
    input_edged = pad_rows(edged[0, :, reach - 1 : reach + col_count + 1])
    hidden_edged = pad_rows(edged[1, :, reach - 1 : reach + col_count + 1])
    feature_wide = conv_cells(pad_rows(edged[1]), conv_weight, wide_cols).astype(jnp.bfloat16)
    owners = owner_strip[0, :, 0]
    strip_ids = jnp.arange(strip_count, dtype=jnp.int32)
    marks = (owners[:, None] == strip_ids[None, :]).astype(jnp.int32)
    before = jnp.cumsum(marks, axis=0) - marks
    position = jnp.sum(before * marks, axis=1)
    slot_index = owners * capacity + position
    cot_rows = jnp.pad(corr_cotangent[0].T, ((0, 0), (0, 128 - taps_total)))
    meta_home = jnp.stack([window_rows[0], window_cols[0] + 3], axis=1)
    payload = jnp.concatenate([queries, cot_rows], axis=1)
    send_payload = (
        jnp.zeros((slot_count, payload.shape[1]), jnp.bfloat16).at[slot_index].set(payload)
    )
    send_meta = jnp.zeros((slot_count, meta_home.shape[1]), jnp.int32).at[slot_index].set(meta_home)
    got_payload, got_meta = (
        lax.all_to_all(send_payload, "lon", split_axis=0, concat_axis=0, tiled=True),
        lax.all_to_all(send_meta, "lon", split_axis=0, concat_axis=0, tiled=True),
    )
    query_slots = got_payload[:, :channels]
    cot_slots = got_payload[:, channels : channels + taps_total]
    block_rows = math.gcd(slot_count, 512)
    block_count = slot_count // block_rows
    feature_flat = feature_wide.reshape(row_count * wide_cols, channels)
    offsets = jnp.arange(WIN, dtype=jnp.int32)
    row_ids = jnp.arange(row_count, dtype=jnp.int32)
    col_ids = jnp.arange(wide_cols, dtype=jnp.int32)

    def block_step(grad_acc, block_items):
        cot_block, meta_block, query_block = block_items
        cot_square = cot_block.reshape(block_rows, WIN, WIN)
        row_hot = (
            meta_block[:, 0][:, None, None] + offsets[None, :, None] == row_ids[None, None, :]
        ).astype(jnp.bfloat16)
        col_hot = (
            meta_block[:, 1][:, None, None] + offsets[None, :, None] == col_ids[None, None, :]
        ).astype(jnp.bfloat16)
        placed_cols = jnp.einsum(
            "tij,tjh->tih", cot_square, col_hot, preferred_element_type=jnp.float32
        ).astype(jnp.bfloat16)
        spread = jnp.einsum(
            "tir,tih->trh", row_hot, placed_cols, preferred_element_type=jnp.float32
        ).astype(jnp.bfloat16)
        spread = spread.reshape(block_rows, row_count * wide_cols)
        block_grads = jnp.dot(spread, feature_flat, preferred_element_type=jnp.float32)
        grad_acc = grad_acc + lax.dot_general(
            spread, query_block, (((0,), (0,)), ((), ())), preferred_element_type=jnp.float32
        )
        return (grad_acc, block_grads)

    block_items = (
        cot_slots.reshape(block_count, block_rows, taps_total),
        got_meta.reshape(block_count, block_rows, got_meta.shape[1]),
        query_slots.reshape(block_count, block_rows, channels),
    )
    grad_flat, query_blocks = lax.scan(
        block_step, jnp.zeros((row_count * wide_cols, channels), jnp.float32), block_items
    )
    slot_grads = query_blocks.reshape(slot_count, channels)
    returned = lax.all_to_all(slot_grads, "lon", split_axis=0, concat_axis=0, tiled=True)
    home_grads = returned[slot_index]
    query_grad = lax.psum_scatter(home_grads, "frame", scatter_dimension=0, tiled=True)
    grad_wide = grad_flat.reshape(row_count, wide_cols, channels)
    from_prior = from_behind(grad_wide[:, col_count + 3 :], "lon", 1)
    from_next = from_behind(grad_wide[:, :3], "lon", -1)
    own_grad = grad_wide[:, 3 : col_count + 3]
    own_grad = own_grad.at[:, :3].add(from_prior)
    own_grad = own_grad.at[:, col_count - 3 :].add(from_next)
    grad_edged = padded_2(own_grad.astype(jnp.bfloat16), (("lon", 1),), 1)
    feature_grad = grad_edged[:, 1 : col_count + 1]
    hidden_grad = conv_back(pad_rows(grad_edged), conv_weight, col_count)
    pre_grad = jnp.where(hidden_local > 0, hidden_grad, jnp.zeros_like(hidden_grad)).astype(
        jnp.bfloat16
    )
    second_term = weight_terms(hidden_edged, feature_grad)
    first_term = weight_terms(input_edged, pre_grad)
    first_sum, second_sum = lax.psum((first_term, second_term), ("lon", "frame"))
    norm_factor = 1.0 / math.sqrt(row_count * col_count * strip_count * lax.axis_size("frame"))
    return (query_grad, first_sum * norm_factor, second_sum * norm_factor)


def solution(mesh):
    placed = (
        P("frame", None, "lon", None),
        P("frame", None, "lon", None),
        P(),
        P("lon", None),
        P("frame", None, "lon"),
        P("frame", "lon"),
        P("frame", "lon"),
        P("frame", "lon", None),
    )
    return jax.shard_map(
        per_device,
        mesh=mesh,
        in_specs=placed,
        out_specs=(P(("lon", "frame"), None), P(), P()),
        check_vma=False,
    )
```

profile of v0, /device:TPU:0, one launch (start us, length us, event | category | flops | bytes accessed | tf_op | source)
XLA Modules:
  0.0 221.2 jit_solution(16327299058159711779)
XLA Ops:
  8.8 1.2 reduce-window.6
  13.4 1.8 scatter_custom_fusion
  15.9 4.2 %all-to-all-start = ((s32[4,128,2]{1,2,0:T(2,128)}), s32[4,128,2]{1,2,0:T(2,128)S(1)}, u32[]{:S(2)}, u32[]{:S(2)}) async-start(s32[4,128,2]{1,2,0:T(2,128)} %copy.76), calls=%async_computation | async-start | bytes 8192 | tf_op jit(solution)/shard_map/all_to_all | solution.py:116
  20.3 1.8 collective-permute-start.1
  22.4 3.0 %scatter_custom_fusion.1 = bf16[512,256]{1,0:T(8,128)(2,1)} fusion(s32[512]{0:T(512)S(1)} %bitcast.248, bf16[512,256]{1,0:T(8,128)(2,1)S(1)} %copy.78, bf16[]{:T(256)} %constant.86.clone.1), kind=kCustom, calls=%fused_computation.147 | custom fusion | bytes 262146 | tf_op jit(solution)/shard_map/scatter | solution.py:111
  25.4 3.4 %all-to-all-start.1 = ((bf16[4,128,256]{2,1,0:T(8,128)(2,1)}), bf16[4,128,256]{2,1,0:T(8,128)(2,1)S(1)}, u32[]{:S(2)}, u32[]{:S(2)}) async-start(bf16[4,128,256]{2,1,0:T(8,128)(2,1)} %bitcast.13), calls=%async_computation.1 | async-start | bytes 524288 | tf_op jit(solution)/shard_map/all_to_all | solution.py:115
  29.9 0.9 copy-done.3
  34.2 1.3 fusion.9
  36.1 5.9 %fusion.1 = bf16[512,16,134]{2,1,0:T(8,128)(2,1)} fusion(bf16[512,7,7]{2,1,0:T(8,128)(2,1)S(1)} %reshape.292, s32[512,7]{1,0:T(8,128)S(1)} %get-tuple-element.69, s32[512,7]{1,0:T(8,128)S(1)} %get-tuple-element.70), kind=kOutput, calls=%fused_computation.5 | convolution fusion | flops 23109632 | bytes 2274304 | tf_op jit(solution)/shard_map/while/body/eval_jaxpr/tir,tih->trh/dot_general | solution.py:139
  42.0 7.9 %copy.81 = bf16[512,16,134]{0,1,2:T(8,128)(2,1)} copy(bf16[512,16,134]{2,1,0:T(8,128)(2,1)} %fusion.1) | data formatting | bytes 4390912 | tf_op jit(solution)/shard_map/while/body/eval_jaxpr/tir,tih->trh/dot_general | solution.py:139
  49.9 2.8 %copy.83 = bf16[512,16,134]{0,2,1:T(8,128)(2,1)S(1)} copy(bf16[512,16,134]{0,1,2:T(8,128)(2,1)} %copy.81) | data formatting | bytes 4390912 | tf_op jit(solution)/shard_map/while/body/eval_jaxpr/convert_element_type | solution.py:141
  52.7 2.1 reshape.236
  54.9 2.6 %dot_general.141 = bf16[16,134,512]{2,1,0:T(8,128)(2,1)S(1)} reshape(bf16[2144,512]{1,0:T(8,128)(2,1)} %bitcast.235) | data formatting | bytes 4390912 | tf_op jit(solution)/shard_map/while/body/eval_jaxpr/dot_general | solution.py:144
  57.5 1.6 fusion.97
  60.2 1.3 collective-permute-start.3
  61.5 1.1 collective-permute-done.2
  63.7 1.8 collective-permute-start.5
  77.5 2.5 %fusion.46 = f32[512,128,1]{1,0,2:T(8,128)} fusion(bf16[512,16,134]{0,1,2:T(8,128)(2,1)S(1)} %copy-done, bf16[16,134,128]{2,1,0:T(8,128)(2,1)} %fusion.9), kind=kOutput, calls=%fused_computation.87 | convolution fusion | flops 281018368 | bytes 3006464 | tf_op jit(solution)/shard_map/while/body/eval_jaxpr/dot_general | solution.py:143
  80.0 3.4 %all-to-all-start.2 = ((f32[4,128,128]{2,1,0:T(8,128)}), f32[4,128,128]{2,1,0:T(8,128)S(1)}, u32[]{:S(2)}, u32[]{:S(2)}) async-start(f32[4,128,128]{2,1,0:T(8,128)} %bitcast.36), calls=%async_computation.2 | async-start | bytes 524288 | tf_op jit(solution)/shard_map/all_to_all | solution.py:158
  83.5 6.6 %all-to-all-done.2 = f32[4,128,128]{2,1,0:T(8,128)S(1)} async-done(((f32[4,128,128]{2,1,0:T(8,128)}), f32[4,128,128]{2,1,0:T(8,128)S(1)}, u32[]{:S(2)}, u32[]{:S(2)}) %all-to-all-start.2) | async-done | bytes 262176 | tf_op jit(solution)/shard_map/all_to_all | solution.py:158
  90.1 1.6 gather_fusion
  91.8 119.1 %all-reduce.8.cloned.1.call-done = (f32[3,3,128,128]{3,2,1,0:T(8,128)}, f32[3,3,128,128]{3,2,1,0:T(8,128)}) async-done(((f32[3,3,128,128]{3,2,1,0:T(8,128)}, f32[3,3,128,128]{3,2,1,0:T(8,128)}), (f32[3,3,128,128]{3,2,1,0:T(8,128)}, f32[3,3,128,128]{3,2,1,0:T(8,128)})) %all-reduce.8.cloned.1.call-update) | async-done | bytes 1179664 | tf_op jit(solution)/shard_map/psum | solution.py:175
  210.9 2.0 broadcast_multiply_fusion.1
  212.9 0.9 broadcast_multiply_fusion
  (106 shorter events, 24.3 us)
Async XLA Ops:
  8.0 12.1 %copy-start.9 = (bf16[1,16,128,128]{3,2,1,0:T(8,128)(2,1)S(1)}, bf16[1,16,128,128]{3,2,1,0:T(8,128)(2,1)}, u32[]{:S(2)}) copy-start(bf16[1,16,128,128]{3,2,1,0:T(8,128)(2,1)} %param.12) | copy-start | bytes 1572868
  8.0 12.2 %copy-start.1 = (bf16[1,16,128,128]{3,2,1,0:T(8,128)(2,1)S(1)}, bf16[1,16,128,128]{3,2,1,0:T(8,128)(2,1)}, u32[]{:S(2)}) copy-start(bf16[1,16,128,128]{3,2,1,0:T(8,128)(2,1)} %param.13) | copy-start | bytes 1572868
  15.9 9.5 %all-to-all-start = ((s32[4,128,2]{1,2,0:T(2,128)}), s32[4,128,2]{1,2,0:T(2,128)S(1)}, u32[]{:S(2)}, u32[]{:S(2)}) async-start(s32[4,128,2]{1,2,0:T(2,128)} %copy.76), calls=%async_computation | async-start | bytes 8192 | tf_op jit(solution)/shard_map/all_to_all | solution.py:116
  20.1 2.0 copy-start.10
  20.1 2.1 copy-start.11
  20.3 9.0 %collective-permute-start.1 = (bf16[2,16,4,128]{3,2,1,0:T(4,128)(2,1)S(1)}, bf16[2,16,4,128]{3,2,1,0:T(4,128)(2,1)S(1)}, u32[]{:S(2)}, u32[]{:S(2)}) collective-permute-start(bf16[2,16,4,128]{3,2,1,0:T(4,128)(2,1)S(1)} %get-tuple-element.64), channel_id=1, source_target_pairs={{8,0},{16,8},{24,16},{0,24},{9,1},{17,9},{25,17},{1,25},{10,2},{18... | collective-permute-start | bytes 98312 | tf_op jit(solution)/shard_map/ppermute | solution.py:18
  22.1 7.2 %collective-permute-start = (bf16[2,16,4,128]{3,2,1,0:T(4,128)(2,1)S(1)}, bf16[2,16,4,128]{3,2,1,0:T(4,128)(2,1)S(1)}, u32[]{:S(2)}, u32[]{:S(2)}) collective-permute-start(bf16[2,16,4,128]{3,2,1,0:T(4,128)(2,1)S(1)} %get-tuple-element.63), channel_id=1, source_target_pairs={{0,8},{8,16},{16,24},{24,0},{1,9},{9,17},{17,25},{25,1},{2,10},{10... | collective-permute-start | bytes 98312 | tf_op jit(solution)/shard_map/ppermute | solution.py:17
  25.4 10.1 %all-to-all-start.1 = ((bf16[4,128,256]{2,1,0:T(8,128)(2,1)}), bf16[4,128,256]{2,1,0:T(8,128)(2,1)S(1)}, u32[]{:S(2)}, u32[]{:S(2)}) async-start(bf16[4,128,256]{2,1,0:T(8,128)(2,1)} %bitcast.13), calls=%async_computation.1 | async-start | bytes 524288 | tf_op jit(solution)/shard_map/all_to_all | solution.py:115
  28.8 182.1 %all-reduce.8.cloned.1.call-start = ((), (), s32[]{:S(2)}) async-start(), calls=%async_computation.5 | async-start | bytes 2359296 | tf_op jit(solution)/shard_map/psum | solution.py:175
  29.8 1.0 copy-start.3
  35.5 6.5 %copy-start.5 = (bf16[4,128,256]{2,1,0:T(8,128)(2,1)}, bf16[4,128,256]{2,1,0:T(8,128)(2,1)S(1)}, u32[]{:S(2)}) copy-start(bf16[4,128,256]{2,1,0:T(8,128)(2,1)S(1)} %all-to-all-done.1) | copy-start | bytes 786436
  59.2 3.4 %collective-permute-start.2 = (f32[16,3,128]{2,1,0:T(4,128)S(1)}, f32[16,3,128]{2,1,0:T(4,128)S(1)}, u32[]{:S(2)}, u32[]{:S(2)}) collective-permute-start(f32[16,3,128]{2,1,0:T(4,128)S(1)} %get-tuple-element.62), channel_id=1, source_target_pairs={{0,8},{8,16},{16,24},{24,0},{1,9},{9,17},{17,25},{25,1},{2,10},{10... | collective-permute-start | bytes 73736 | tf_op jit(solution)/shard_map/ppermute | solution.py:26
  60.2 3.2 %copy-start.4 = (bf16[3,3,128,128]{3,2,1,0:T(8,128)(2,1)S(1)}, bf16[3,3,128,128]{3,2,1,0:T(8,128)(2,1)}, u32[]{:S(2)}) copy-start(bf16[3,3,128,128]{3,2,1,0:T(8,128)(2,1)} %param.14) | copy-start | bytes 884740
  60.2 2.9 %collective-permute-start.3 = (f32[16,3,128]{2,1,0:T(4,128)S(1)}, f32[16,3,128]{2,1,0:T(4,128)S(1)}, u32[]{:S(2)}, u32[]{:S(2)}) collective-permute-start(f32[16,3,128]{2,1,0:T(4,128)S(1)} %get-tuple-element.61), channel_id=1, source_target_pairs={{0,24},{8,0},{16,8},{24,16},{1,25},{9,1},{17,9},{25,17},{2,26},{10... | collective-permute-start | bytes 73736 | tf_op jit(solution)/shard_map/ppermute | solution.py:26
  63.7 5.4 %collective-permute-start.5 = (bf16[16,1,128]{2,1,0:T(2,128)(2,1)S(1)}, bf16[16,1,128]{2,1,0:T(2,128)(2,1)S(1)}, u32[]{:S(2)}, u32[]{:S(2)}) collective-permute-start(bf16[16,1,128]{2,1,0:T(2,128)(2,1)S(1)} %get-tuple-element.66), channel_id=1, source_target_pairs={{8,0},{16,8},{24,16},{0,24},{9,1},{17,9},{25,17},{1,25},{10,2},{18... | collective-permute-start | bytes 12296 | tf_op jit(solution)/shard_map/ppermute | solution.py:18
  65.5 3.6 %collective-permute-start.4 = (bf16[16,1,128]{2,1,0:T(2,128)(2,1)S(1)}, bf16[16,1,128]{2,1,0:T(2,128)(2,1)S(1)}, u32[]{:S(2)}, u32[]{:S(2)}) collective-permute-start(bf16[16,1,128]{2,1,0:T(2,128)(2,1)S(1)} %get-tuple-element.65), channel_id=1, source_target_pairs={{0,8},{8,16},{16,24},{24,0},{1,9},{9,17},{17,25},{25,1},{2,10},{10... | collective-permute-start | bytes 12296 | tf_op jit(solution)/shard_map/ppermute | solution.py:17
  69.1 0.8 copy-start.6
  71.5 1.0 copy-start.2
  75.6 1.8 copy-start
  76.0 0.8 copy-start.7
  80.0 10.1 %all-to-all-start.2 = ((f32[4,128,128]{2,1,0:T(8,128)}), f32[4,128,128]{2,1,0:T(8,128)S(1)}, u32[]{:S(2)}, u32[]{:S(2)}) async-start(f32[4,128,128]{2,1,0:T(8,128)} %bitcast.36), calls=%async_computation.2 | async-start | bytes 524288 | tf_op jit(solution)/shard_map/all_to_all | solution.py:158
  83.4 130.3 %reduce-scatter.2.cloned.1.call-start = ((), (), s32[]{:S(2)}) async-start(), calls=%async_computation.4 | async-start | bytes 294912 | tf_op jit(solution)/shard_map/reduce_scatter | solution.py:160
  210.9 2.0 copy-start.8
Sparse Core Ops, SparseCore 0:
  77.0 133.8 all-reduce.7
Sparse Core Ops, SparseCore 1:
  91.8 62.9 reduce-scatter.1
where the time goes:
time: 222 us; the launch traced here: 221 us
  waiting for transfers between devices  127 us (57%)
  local copies, waits for them, and re-layouts  28.2 us (13%)
  matrix products  23.8 us (11%)
  starting transfers between devices  17.2 us (8%)
  between operations  16 us (7%)
  other arithmetic  8.87 us (4%)
    psum x1, waiting for transfers between devices, per_device(): lax.psum((first_term, second_term), ('lon', 'frame'))  119 us
    dot_general x1, local copies, waits for them, and re-layouts, block_step(): jnp.einsum('tir,tih->trh', row_hot, placed_cols, preferred_element_type=j...  7.86 us
    all_to_all x1, waiting for transfers between devices, per_device(): lax.all_to_all(slot_grads, 'lon', split_axis=0, concat_axis=0, tiled=True)  6.61 us
    dot_general x18, matrix products, weight_terms(): lax.dot_general(window, flat_grad, (((0,), (0,)), ((), ())), preferred_el...  6.16 us
    dot_general x1, matrix products, block_step(): jnp.einsum('tir,tih->trh', row_hot, placed_cols, preferred_element_type=j...  5.92 us
    dot_general x9, matrix products, conv_cells(): jnp.einsum('rci,io->rco', window, weight[row_tap, col_tap], preferred_ele...  4.72 us
  transfers between devices with their start and end apart: 11, of which 4 were waited for; matrix products, arithmetic and copies ran while one was open for 9% of the time, Pallas kernels for 0%

commit v1 on v0

--- a/solution.py
+++ b/solution.py
@@ -5,6 +5,12 @@
 from jax.sharding import PartitionSpec as P
 
 WIN = 7
+
+
+def group_solve(original):
+    current_block = jax.lax.psum(original, axis_name="frame")
+    even = jax.lax.psum(current_block, axis_name="lon")
+    return even
 
 
 def padded_2(value, sides, width):
@@ -172,7 +178,7 @@
     )
     second_term = weight_terms(hidden_edged, feature_grad)
     first_term = weight_terms(input_edged, pre_grad)
-    first_sum, second_sum = lax.psum((first_term, second_term), ("lon", "frame"))
+    first_sum, second_sum = group_solve((first_term, second_term))
     norm_factor = 1.0 / math.sqrt(row_count * col_count * strip_count * lax.axis_size("frame"))
     return (query_grad, first_sum * norm_factor, second_sum * norm_factor)
 

time: 222 us -> 275 us (1.24)
  waiting for transfers between devices: 127 us -> 175 us
  matrix products: 23.8 us -> 27.9 us
    reduce_scatter x1, waiting for transfers between devices: 0.01 us -> 63.3 us  [per_device(): lax.psum_scatter(home_grads, 'frame', scatter_dimension=0, tiled=True)]
    psum x1 -> x2, waiting for transfers between devices: 119 us -> 103 us  [the longest x1 78.6 us: group_solve(): current_block = jax.lax.psum(original, axis_name='frame')]
    dot_general x9, matrix products: 4.72 us -> 9.68 us  [conv_cells(): jnp.einsum('rci,io->rco', window, weight[row_tap, col_tap], preferred_ele...]
  transfers between devices with their start and end apart: 11 -> 12, of which waited for: 4 -> 5; matrix products, arithmetic and copies ran while one was open for 9% -> 9% of each run, Pallas kernels for 0% -> 0%
where the time goes in v1:
time: 275 us; the launch traced here: 274 us
  waiting for transfers between devices  175 us (64%)
  local copies, waits for them, and re-layouts  28.7 us (10%)
  matrix products  27.9 us (10%)
  starting transfers between devices  16.6 us (6%)
  between operations  14.3 us (5%)
  other arithmetic  10.9 us (4%)
    psum x1, waiting for transfers between devices, group_solve(): current_block = jax.lax.psum(original, axis_name='frame')  78.6 us
    reduce_scatter x1, waiting for transfers between devices, per_device(): lax.psum_scatter(home_grads, 'frame', scatter_dimension=0, tiled=True)  63.3 us
    psum x1, waiting for transfers between devices, group_solve(): even = jax.lax.psum(current_block, axis_name='lon')  24.2 us
    dot_general x9, matrix products, conv_cells(): jnp.einsum('rci,io->rco', window, weight[row_tap, col_tap], preferred_ele...  9.68 us
    all_to_all x1, waiting for transfers between devices, per_device(): lax.all_to_all(slot_grads, 'lon', split_axis=0, concat_axis=0, tiled=True)  8.4 us
    dot_general x1, local copies, waits for them, and re-layouts, block_step(): jnp.einsum('tir,tih->trh', row_hot, placed_cols, preferred_element_type=j...  7.87 us
    dot_general x18, matrix products, weight_terms(): lax.dot_general(window, flat_grad, (((0,), (0,)), ((), ())), preferred_el...  6.14 us
    dot_general x1, matrix products, block_step(): jnp.einsum('tir,tih->trh', row_hot, placed_cols, preferred_element_type=j...  5.9 us
  transfers between devices with their start and end apart: 12, of which 5 were waited for; matrix products, arithmetic and copies ran while one was open for 9% of the time, Pallas kernels for 0%

profile of v1, /device:TPU:0, one launch (start us, length us, event | category | flops | bytes accessed | tf_op | source)
XLA Modules:
  0.0 273.7 jit_solution(3359956333663298119)
XLA Ops:
  12.6 1.8 scatter_custom_fusion
  15.1 4.2 %all-to-all-start = ((s32[4,128,2]{1,2,0:T(2,128)}), s32[4,128,2]{1,2,0:T(2,128)S(1)}, u32[]{:S(2)}, u32[]{:S(2)}) async-start(s32[4,128,2]{1,2,0:T(2,128)} %copy.76), calls=%async_computation | async-start | bytes 8192 | tf_op jit(solution)/shard_map/all_to_all | solution.py:122
  19.5 1.8 collective-permute-start.1
  21.6 3.0 %scatter_custom_fusion.1 = bf16[512,256]{1,0:T(8,128)(2,1)} fusion(s32[512]{0:T(512)S(1)} %bitcast.248, bf16[512,256]{1,0:T(8,128)(2,1)S(1)} %copy.78, bf16[]{:T(256)} %constant.86.clone.1), kind=kCustom, calls=%fused_computation.147 | custom fusion | bytes 262146 | tf_op jit(solution)/shard_map/scatter | solution.py:117
  24.6 3.4 %all-to-all-start.1 = ((bf16[4,128,256]{2,1,0:T(8,128)(2,1)}), bf16[4,128,256]{2,1,0:T(8,128)(2,1)S(1)}, u32[]{:S(2)}, u32[]{:S(2)}) async-start(bf16[4,128,256]{2,1,0:T(8,128)(2,1)} %bitcast.13), calls=%async_computation.1 | async-start | bytes 524288 | tf_op jit(solution)/shard_map/all_to_all | solution.py:121
  32.5 2.2 convolution_add_fusion.5
  36.0 5.9 %fusion.1 = bf16[512,16,134]{2,1,0:T(8,128)(2,1)} fusion(bf16[512,7,7]{2,1,0:T(8,128)(2,1)S(1)} %reshape.292, s32[512,7]{1,0:T(8,128)S(1)} %get-tuple-element.71, s32[512,7]{1,0:T(8,128)S(1)} %get-tuple-element.72), kind=kOutput, calls=%fused_computation.5 | convolution fusion | flops 23109632 | bytes 2274304 | tf_op jit(solution)/shard_map/while/body/eval_jaxpr/tir,tih->trh/dot_general | solution.py:145
  41.9 7.9 %copy.81 = bf16[512,16,134]{0,1,2:T(8,128)(2,1)} copy(bf16[512,16,134]{2,1,0:T(8,128)(2,1)} %fusion.1) | data formatting | bytes 4390912 | tf_op jit(solution)/shard_map/while/body/eval_jaxpr/tir,tih->trh/dot_general | solution.py:145
  49.7 2.8 %copy.83 = bf16[512,16,134]{0,2,1:T(8,128)(2,1)S(1)} copy(bf16[512,16,134]{0,1,2:T(8,128)(2,1)} %copy.81) | data formatting | bytes 4390912 | tf_op jit(solution)/shard_map/while/body/eval_jaxpr/convert_element_type | solution.py:147
  52.6 2.1 reshape.236
  54.7 2.6 dot_general.141
  57.3 1.7 fusion.97
  60.7 1.5 collective-permute-start.3
  64.6 1.4 slice_add_fusion
  67.3 1.3 collective-permute-start.5
  81.0 2.2 fusion.9
  83.2 78.6 %all-reduce.10.cloned.1.call-done = (f32[3,3,128,128]{3,2,1,0:T(8,128)}, f32[3,3,128,128]{3,2,1,0:T(8,128)}) async-done(((f32[3,3,128,128]{3,2,1,0:T(8,128)}, f32[3,3,128,128]{3,2,1,0:T(8,128)}), (f32[3,3,128,128]{3,2,1,0:T(8,128)}, f32[3,3,128,128]{3,2,1,0:T(8,128)})) %all-reduce.10.cloned.1.call-update) | async-done | bytes 1179664 | tf_op jit(solution)/shard_map/psum | solution.py:11
  161.9 1.5 fusion.46
  163.3 3.4 %all-to-all-start.2 = ((f32[4,128,128]{2,1,0:T(8,128)}), f32[4,128,128]{2,1,0:T(8,128)S(1)}, u32[]{:S(2)}, u32[]{:S(2)}) async-start(f32[4,128,128]{2,1,0:T(8,128)} %bitcast.36), calls=%async_computation.2 | async-start | bytes 524288 | tf_op jit(solution)/shard_map/all_to_all | solution.py:164
  166.8 8.4 %all-to-all-done.2 = f32[4,128,128]{2,1,0:T(8,128)S(1)} async-done(((f32[4,128,128]{2,1,0:T(8,128)}), f32[4,128,128]{2,1,0:T(8,128)S(1)}, u32[]{:S(2)}, u32[]{:S(2)}) %all-to-all-start.2) | async-done | bytes 262176 | tf_op jit(solution)/shard_map/all_to_all | solution.py:164
  175.2 1.6 gather_fusion
  176.9 24.2 %all-reduce.12.cloned.1.call-done = (f32[3,3,128,128]{3,2,1,0:T(8,128)}, f32[3,3,128,128]{3,2,1,0:T(8,128)}) async-done(((f32[3,3,128,128]{3,2,1,0:T(8,128)}, f32[3,3,128,128]{3,2,1,0:T(8,128)}), (f32[3,3,128,128]{3,2,1,0:T(8,128)}, f32[3,3,128,128]{3,2,1,0:T(8,128)})) %all-reduce.12.cloned.1.call-update) | async-done | bytes 1179664 | tf_op jit(solution)/shard_map/psum | solution.py:12
  201.0 2.0 broadcast_multiply_fusion.1
  203.9 63.3 %reduce-scatter.2.cloned.1.call-done = f32[64,128]{1,0:T(8,128)} async-done(((f32[512,128]{1,0:T(8,128)}), f32[64,128]{1,0:T(8,128)}) %reduce-scatter.2.cloned.1.call-update) | async-done | bytes 32784 | tf_op jit(solution)/shard_map/reduce_scatter | solution.py:166
  (113 shorter events, 30.7 us)
Async XLA Ops:
  7.2 12.1 %copy-start.11 = (bf16[1,16,128,128]{3,2,1,0:T(8,128)(2,1)S(1)}, bf16[1,16,128,128]{3,2,1,0:T(8,128)(2,1)}, u32[]{:S(2)}) copy-start(bf16[1,16,128,128]{3,2,1,0:T(8,128)(2,1)} %param.12) | copy-start | bytes 1572868
  7.2 12.2 %copy-start.4 = (bf16[1,16,128,128]{3,2,1,0:T(8,128)(2,1)S(1)}, bf16[1,16,128,128]{3,2,1,0:T(8,128)(2,1)}, u32[]{:S(2)}) copy-start(bf16[1,16,128,128]{3,2,1,0:T(8,128)(2,1)} %param.13) | copy-start | bytes 1572868
  15.1 9.5 %all-to-all-start = ((s32[4,128,2]{1,2,0:T(2,128)}), s32[4,128,2]{1,2,0:T(2,128)S(1)}, u32[]{:S(2)}, u32[]{:S(2)}) async-start(s32[4,128,2]{1,2,0:T(2,128)} %copy.76), calls=%async_computation | async-start | bytes 8192 | tf_op jit(solution)/shard_map/all_to_all | solution.py:122
  19.3 2.0 copy-start.12
  19.3 2.1 copy-start.13
  19.5 8.8 %collective-permute-start.1 = (bf16[2,16,4,128]{3,2,1,0:T(4,128)(2,1)S(1)}, bf16[2,16,4,128]{3,2,1,0:T(4,128)(2,1)S(1)}, u32[]{:S(2)}, u32[]{:S(2)}) collective-permute-start(bf16[2,16,4,128]{3,2,1,0:T(4,128)(2,1)S(1)} %get-tuple-element.66), channel_id=1, source_target_pairs={{8,0},{16,8},{24,16},{0,24},{9,1},{17,9},{25,17},{1,25},{10,2},{18... | collective-permute-start | bytes 98312 | tf_op jit(solution)/shard_map/ppermute | solution.py:24
  21.3 7.0 %collective-permute-start = (bf16[2,16,4,128]{3,2,1,0:T(4,128)(2,1)S(1)}, bf16[2,16,4,128]{3,2,1,0:T(4,128)(2,1)S(1)}, u32[]{:S(2)}, u32[]{:S(2)}) collective-permute-start(bf16[2,16,4,128]{3,2,1,0:T(4,128)(2,1)S(1)} %get-tuple-element.65), channel_id=1, source_target_pairs={{0,8},{8,16},{16,24},{24,0},{1,9},{9,17},{17,25},{25,1},{2,10},{10... | collective-permute-start | bytes 98312 | tf_op jit(solution)/shard_map/ppermute | solution.py:23
  24.6 10.1 %all-to-all-start.1 = ((bf16[4,128,256]{2,1,0:T(8,128)(2,1)}), bf16[4,128,256]{2,1,0:T(8,128)(2,1)S(1)}, u32[]{:S(2)}, u32[]{:S(2)}) async-start(bf16[4,128,256]{2,1,0:T(8,128)(2,1)} %bitcast.13), calls=%async_computation.1 | async-start | bytes 524288 | tf_op jit(solution)/shard_map/all_to_all | solution.py:121
  28.0 133.8 %all-reduce.10.cloned.1.call-start = ((), (), s32[]{:S(2)}) async-start(), calls=%async_computation.5 | async-start | bytes 2359296 | tf_op jit(solution)/shard_map/psum | solution.py:11
  28.8 1.3 copy-start.1
  57.3 2.9 %copy-start.2 = (bf16[2,16,136,128]{3,2,1,0:T(8,128)(2,1)S(1)}, bf16[2,16,136,128]{3,2,1,0:T(8,128)(2,1)}, u32[]{:S(2)}) copy-start(bf16[2,16,136,128]{3,2,1,0:T(8,128)(2,1)} %copy-done.1) | copy-start | bytes 3342340
  59.7 3.3 %collective-permute-start.2 = (f32[16,3,128]{2,1,0:T(4,128)S(1)}, f32[16,3,128]{2,1,0:T(4,128)S(1)}, u32[]{:S(2)}, u32[]{:S(2)}) collective-permute-start(f32[16,3,128]{2,1,0:T(4,128)S(1)} %get-tuple-element.64), channel_id=1, source_target_pairs={{0,8},{8,16},{16,24},{24,0},{1,9},{9,17},{17,25},{25,1},{2,10},{10... | collective-permute-start | bytes 73736 | tf_op jit(solution)/shard_map/ppermute | solution.py:32
  60.7 6.3 %copy-start.5 = (bf16[3,3,128,128]{3,2,1,0:T(8,128)(2,1)S(1)}, bf16[3,3,128,128]{3,2,1,0:T(8,128)(2,1)}, u32[]{:S(2)}) copy-start(bf16[3,3,128,128]{3,2,1,0:T(8,128)(2,1)} %param.14) | copy-start | bytes 884740
  60.7 3.9 %collective-permute-start.3 = (f32[16,3,128]{2,1,0:T(4,128)}, f32[16,3,128]{2,1,0:T(4,128)}, u32[]{:S(2)}, u32[]{:S(2)}) collective-permute-start(f32[16,3,128]{2,1,0:T(4,128)} %get-tuple-element.63), channel_id=1, source_target_pairs={{0,24},{8,0},{16,8},{24,16},{1,25},{9,1},{17,9},{25,17},{2,26},{10... | collective-permute-start | bytes 73736 | tf_op jit(solution)/shard_map/ppermute | solution.py:32
  67.3 4.8 %collective-permute-start.5 = (bf16[16,1,128]{2,1,0:T(2,128)(2,1)S(1)}, bf16[16,1,128]{2,1,0:T(2,128)(2,1)S(1)}, u32[]{:S(2)}, u32[]{:S(2)}) collective-permute-start(bf16[16,1,128]{2,1,0:T(2,128)(2,1)S(1)} %get-tuple-element.68), channel_id=1, source_target_pairs={{8,0},{16,8},{24,16},{0,24},{9,1},{17,9},{25,17},{1,25},{10,2},{18... | collective-permute-start | bytes 12296 | tf_op jit(solution)/shard_map/ppermute | solution.py:24
  68.6 3.5 %collective-permute-start.4 = (bf16[16,1,128]{2,1,0:T(2,128)(2,1)S(1)}, bf16[16,1,128]{2,1,0:T(2,128)(2,1)S(1)}, u32[]{:S(2)}, u32[]{:S(2)}) collective-permute-start(bf16[16,1,128]{2,1,0:T(2,128)(2,1)S(1)} %get-tuple-element.67), channel_id=1, source_target_pairs={{0,8},{8,16},{16,24},{24,0},{1,9},{9,17},{17,25},{25,1},{2,10},{10... | collective-permute-start | bytes 12296 | tf_op jit(solution)/shard_map/ppermute | solution.py:23
  72.1 0.8 copy-start.7
  78.0 1.3 copy-start.3
  79.2 121.9 %all-reduce.12.cloned.1.call-start = ((), (), s32[]{:S(2)}) async-start(), calls=%async_computation.6 | async-start | bytes 2359296 | tf_op jit(solution)/shard_map/psum | solution.py:12
  81.0 80.8 %copy-start = (bf16[512,16,134]{0,1,2:T(8,128)(2,1)S(1)}, bf16[512,16,134]{0,1,2:T(8,128)(2,1)}, u32[]{:S(2)}) copy-start(bf16[512,16,134]{0,1,2:T(8,128)(2,1)} %copy.81) | copy-start | bytes 6586372
  83.2 78.7 %copy-start.10 = (bf16[16,134,128]{2,1,0:T(8,128)(2,1)S(1)}, bf16[16,134,128]{2,1,0:T(8,128)(2,1)}, u32[]{:S(2)}) copy-start(bf16[16,134,128]{2,1,0:T(8,128)(2,1)} %fusion.9) | copy-start | bytes 1646596
  163.3 11.9 %all-to-all-start.2 = ((f32[4,128,128]{2,1,0:T(8,128)}), f32[4,128,128]{2,1,0:T(8,128)S(1)}, u32[]{:S(2)}, u32[]{:S(2)}) async-start(f32[4,128,128]{2,1,0:T(8,128)} %bitcast.36), calls=%async_computation.2 | async-start | bytes 524288 | tf_op jit(solution)/shard_map/all_to_all | solution.py:164
  166.8 100.5 %reduce-scatter.2.cloned.1.call-start = ((), (), s32[]{:S(2)}) async-start(), calls=%async_computation.4 | async-start | bytes 294912 | tf_op jit(solution)/shard_map/reduce_scatter | solution.py:166
  201.0 2.0 copy-start.9
  (2 other events, 1.5 us)
Sparse Core Ops, SparseCore 0:
  79.3 82.4 all-reduce.9
  164.2 36.7 all-reduce.11
  204.9 62.2 reduce-scatter.1
